TPU v7x, 32 devices: a whole 2x2x4 slice. The times are simulated.
32 devices in a mesh: shard: 2 (over x), ctx: 4 (over y, core), tp: 4 (over z).
Axes of the slice: x: 2, y: 2, z: 4, core: 2. Of those that a mesh axis runs over, the one named last changes fastest.
Arguments:
- tokens: bfloat16 [8, 1024, 767], P('shard', 'ctx'), may hold values from -6 to 6
- lengths: int32 [8], P('shard'), may hold values from 256 to 1024, as said below
- first_gain: float32 [768], replicated, may hold values from 0.5 to 1.5
- entry_weight: bfloat16 [3, 768, 768], P(None, ('shard', 'ctx'), 'tp'), may hold values from -0.21875 to 0.21875
- entry_bias: float32 [2, 768], P(None, 'tp'), may hold values from -3 to 3
- exit_weight: bfloat16 [768, 768], P('tp', ('shard', 'ctx')), may hold values from -0.625 to 0.625
- exit_bias: float32 [768], replicated, may hold values from -3 to 3
- second_gain: float32 [768], replicated, may hold values from 0.5 to 1.5
- hidden_weight: bfloat16 [768, 3072], P(('shard', 'ctx'), 'tp'), may hold values from -0.21875 to 0.21875
- hidden_bias: float32 [3072], P('tp'), may hold values from -3 to 3
- return_weight: bfloat16 [3072, 768], P('tp', ('shard', 'ctx')), may hold values from -0.109375 to 0.109375
- return_bias: float32 [768], replicated, may hold values from -3 to 3
- cotangent: bfloat16 [8, 1024, 767], P('shard', 'ctx'), may hold values from -6 to 6
Outputs:
- result: bfloat16 [8, 1024, 767], P('shard', 'ctx')
- tokens_gradient: bfloat16 [8, 1024, 767], P('shard', 'ctx')
- first_gain_gradient: float32 [768], replicated
- entry_weight_gradient: float32 [3, 768, 768], P(None, ('shard', 'ctx'), 'tp')
- entry_bias_gradient: float32 [2, 768], P(None, 'tp')
- exit_weight_gradient: float32 [768, 768], P('tp', ('shard', 'ctx'))
- exit_bias_gradient: float32 [768], replicated
- second_gain_gradient: float32 [768], replicated
- hidden_weight_gradient: float32 [768, 3072], P(('shard', 'ctx'), 'tp')
- hidden_bias_gradient: float32 [3072], P('tp')
- return_weight_gradient: float32 [3072, 768], P('tp', ('shard', 'ctx'))
- return_bias_gradient: float32 [768], replicated
Inputs may be any that keep to these rules, and one draw needn't show every extreme that they name: `lengths`: in every draw some sequence has exactly 1024 valid positions and some has exactly 256.
All inputs are finite; a program needn't handle non-finite values.
Results may differ from a plain program's by a relative error of at most 0.014.
Values may be sent and summed in bfloat16 or wider, within the bound.
No kernel may reach another device: no remote copies, remote signals or barrier semaphores. Data moves between devices by JAX's collectives and lax.ppermute only.
A program may use at most 256 MiB of HBM per device.

v0:
```python
import math
import jax
import jax.numpy as jnp
from jax import lax
from jax.sharding import PartitionSpec as P

HDIM = 64
EPSILON = 1e-05


def row_mean(values):
    return jnp.mean(values, -1, keepdims=True)


def shards(
    tokens,
    lengths,
    first_gain,
    entry_weight,
    entry_bias,
    exit_weight,
    exit_bias,
    second_gain,
    hidden_weight,
    hidden_bias,
    return_weight,
    return_bias,
    cotangent,
):
    seq_dev, local, narrow = tokens.shape
    row_count = seq_dev * local
    full_len = local * lax.axis_size("ctx")
    head_width = entry_weight.shape[2]
    heads_here = head_width // HDIM
    scale = 1.0 / math.sqrt(HDIM)
    bfloat = jnp.bfloat16
    single = jnp.float32
    full_entry, full_exit, full_hidden, full_return = (
        lax.all_gather(entry_weight, ("shard", "ctx"), axis=1, tiled=True),
        lax.all_gather(exit_weight, ("shard", "ctx"), axis=1, tiled=True),
        lax.all_gather(hidden_weight, ("shard", "ctx"), axis=0, tiled=True),
        lax.all_gather(return_weight, ("shard", "ctx"), axis=1, tiled=True),
    )
    stream_part = tokens.astype(single).reshape(row_count, narrow)
    stream = jnp.concatenate([stream_part, -jnp.sum(stream_part, -1, keepdims=True)], 1)
    first_inverse = lax.rsqrt(row_mean(stream * stream) + EPSILON)
    first_unit = stream * first_inverse
    first_normed = (first_unit * first_gain).astype(bfloat)
    queries = (
        jnp.dot(first_normed, full_entry[0], preferred_element_type=single) + entry_bias[0]
    ).astype(bfloat)
    keys = jnp.dot(first_normed, full_entry[1], preferred_element_type=single).astype(bfloat)
    values = (
        jnp.dot(first_normed, full_entry[2], preferred_element_type=single) + entry_bias[1]
    ).astype(bfloat)
    seq_shape = (seq_dev, local, head_width)
    all_keys, all_values = (
        lax.all_gather(keys.reshape(seq_shape), "ctx", axis=1, tiled=True),
        lax.all_gather(values.reshape(seq_shape), "ctx", axis=1, tiled=True),
    )
    offset = lax.axis_index("ctx") * local
    query_pos = offset + jnp.arange(local, dtype=jnp.int32)
    key_pos = jnp.arange(full_len, dtype=jnp.int32)
    local_heads = (seq_dev, local, heads_here, HDIM)
    full_heads = (seq_dev, full_len, heads_here, HDIM)
    allowed = (
        (key_pos[None, None, :] <= query_pos[None, :, None])
        & (key_pos[None, None, :] < lengths[:, None, None])
    )[:, None]

    def masked_scores(query_block, key_block):
        raw_scores = (
            jnp.einsum("sqhd,skhd->shqk", query_block, key_block, preferred_element_type=single)
            * scale
        )
        return jnp.where(allowed, raw_scores, -1e30)

    query_heads = queries.reshape(local_heads)
    scores = masked_scores(query_heads, all_keys.reshape(full_heads))
    largest = jnp.max(scores, -1, keepdims=True)
    exponent = jnp.exp(scores - largest)
    totals = jnp.sum(exponent, -1, keepdims=True)
    weights = (exponent / totals).astype(bfloat)
    log_totals = largest + jnp.log(totals)
    attended = jnp.einsum(
        "shqk,skhd->sqhd", weights, all_values.reshape(full_heads), preferred_element_type=single
    ).astype(bfloat)
    attended_rows = attended.reshape(row_count, head_width)
    exit_term = jnp.dot(attended_rows, full_exit, preferred_element_type=single)
    branch = lax.psum(exit_term, "tp") + exit_bias
    middle = stream + branch - row_mean(branch)
    second_inverse = lax.rsqrt(row_mean(middle * middle) + EPSILON)
    second_unit = middle * second_inverse
    second_normed = (second_unit * second_gain).astype(bfloat)
    hidden = jnp.dot(second_normed, full_hidden, preferred_element_type=single) + hidden_bias
    activated, gelu_pull = jax.vjp(
        lambda values_in: jax.nn.gelu(values_in, approximate=True), hidden
    )
    activated_low = activated.astype(bfloat)
    return_term = jnp.dot(activated_low, full_return, preferred_element_type=single)
    returned = lax.psum(return_term.astype(jnp.bfloat16), "tp").astype(jnp.float32) + return_bias
    full_stream = middle + returned - row_mean(returned)
    result_rows = full_stream[:, :narrow].astype(bfloat)
    result = result_rows.reshape(seq_dev, local, narrow)
    full_entry, full_exit, full_hidden, full_return = (
        lax.all_gather(entry_weight, ("shard", "ctx"), axis=1, tiled=True),
        lax.all_gather(exit_weight, ("shard", "ctx"), axis=1, tiled=True),
        lax.all_gather(hidden_weight, ("shard", "ctx"), axis=0, tiled=True),
        lax.all_gather(return_weight, ("shard", "ctx"), axis=1, tiled=True),
    )
    valid = (query_pos[None, :] < lengths[:, None]).astype(single).reshape(row_count, 1)
    cot_rows = cotangent.astype(single).reshape(row_count, narrow) * valid
    cot_full = jnp.concatenate([cot_rows, jnp.zeros((row_count, 1), single)], 1)
    returned_grad = (cot_full - row_mean(cot_full)).astype(bfloat)
    return_bias_grad = jnp.sum(returned_grad.astype(single), 0)
    return_weight_grad = jnp.einsum(
        "rf,rd->fd", activated_low, returned_grad, preferred_element_type=single
    )
    activated_grad = jnp.einsum(
        "rd,fd->rf", returned_grad, full_return, preferred_element_type=single
    )
    hidden_grad = gelu_pull(activated_grad)[0].astype(bfloat)
    hidden_bias_grad = jnp.sum(hidden_grad.astype(single), 0)
    hidden_weight_grad = jnp.einsum(
        "rd,rf->df", second_normed, hidden_grad, preferred_element_type=single
    )
    second_term = jnp.einsum("rf,df->rd", hidden_grad, full_hidden, preferred_element_type=single)
    second_grad = lax.psum(second_term, "tp")
    second_gain_grad = jnp.sum(second_grad * second_unit, 0)
    second_scaled = second_grad * second_gain
    middle_grad = cot_full + second_inverse * (
        second_scaled - second_unit * row_mean(second_scaled * second_unit)
    )
    branch_grad = (middle_grad - row_mean(middle_grad)).astype(bfloat)
    exit_bias_grad = jnp.sum(branch_grad.astype(single), 0)
    exit_weight_grad = jnp.einsum(
        "re,rd->ed", attended_rows, branch_grad, preferred_element_type=single
    )
    attended_grad = jnp.einsum(
        "rd,ed->re", branch_grad, full_exit, preferred_element_type=single
    ).astype(bfloat)
    all_keys, all_values = (
        lax.all_gather(keys.reshape(seq_shape), "ctx", axis=1, tiled=True),
        lax.all_gather(values.reshape(seq_shape), "ctx", axis=1, tiled=True),
    )
    key_heads = all_keys.reshape(full_heads)
    value_heads = all_values.reshape(full_heads)
    out_grad = attended_grad.reshape(local_heads)
    back_scores = masked_scores(query_heads, key_heads)
    probs = jnp.exp(back_scores - log_totals)
    probs_low = probs.astype(bfloat)
    prob_rounded = lax.optimization_barrier(
        jnp.einsum("sqhd,skhd->shqk", out_grad, value_heads, preferred_element_type=single).astype(
            bfloat
        )
    )
    prob_grad = prob_rounded.astype(single)
    inner = jnp.sum(probs * prob_grad, -1, keepdims=True)
    score_grad = (probs * (prob_grad - inner)).astype(bfloat)
    query_grads = (
        jnp.einsum("shqk,skhd->sqhd", score_grad, key_heads, preferred_element_type=single) * scale
    ).astype(bfloat)
    key_parts = (
        jnp.einsum("shqk,sqhd->skhd", score_grad, query_heads, preferred_element_type=single)
        * scale
    )
    value_parts = jnp.einsum("shqk,sqhd->skhd", probs_low, out_grad, preferred_element_type=single)
    key_sums, value_sums = (
        lax.psum_scatter(
            key_parts.reshape(seq_dev, full_len, head_width), "ctx", scatter_dimension=1, tiled=True
        ),
        lax.psum_scatter(
            value_parts.reshape(seq_dev, full_len, head_width),
            "ctx",
            scatter_dimension=1,
            tiled=True,
        ),
    )
    query_low = query_grads.reshape(row_count, head_width)
    key_low = key_sums.reshape(row_count, head_width).astype(bfloat)
    value_low = value_sums.reshape(row_count, head_width).astype(bfloat)
    entry_bias_grad = jnp.stack(
        [jnp.sum(query_low.astype(single), 0), jnp.sum(value_low.astype(single), 0)]
    )
    entry_weight_grad = jnp.stack(
        [
            jnp.einsum("rd,re->de", first_normed, query_low, preferred_element_type=single),
            jnp.einsum("rd,re->de", first_normed, key_low, preferred_element_type=single),
            jnp.einsum("rd,re->de", first_normed, value_low, preferred_element_type=single),
        ]
    )
    first_part = (
        jnp.einsum("re,de->rd", query_low, full_entry[0], preferred_element_type=single)
        + jnp.einsum("re,de->rd", key_low, full_entry[1], preferred_element_type=single)
        + jnp.einsum("re,de->rd", value_low, full_entry[2], preferred_element_type=single)
    )
    first_grad = lax.psum(first_part, "tp")
    first_gain_grad = jnp.sum(first_grad * first_unit, 0)
    first_scaled = first_grad * first_gain
    stream_grad = middle_grad + first_inverse * (
        first_scaled - first_unit * row_mean(first_scaled * first_unit)
    )
    tokens_rows = (stream_grad[:, :narrow] - stream_grad[:, narrow:]).astype(bfloat)
    tokens_grad = tokens_rows.reshape(seq_dev, local, narrow)
    weight_grads = (
        lax.psum_scatter(entry_weight_grad, ("shard", "ctx"), scatter_dimension=1, tiled=True),
        lax.psum_scatter(exit_weight_grad, ("shard", "ctx"), scatter_dimension=1, tiled=True),
        lax.psum_scatter(hidden_weight_grad, ("shard", "ctx"), scatter_dimension=0, tiled=True),
        lax.psum_scatter(return_weight_grad, ("shard", "ctx"), scatter_dimension=1, tiled=True),
    )
    small_grads = lax.psum(
        (
            first_gain_grad,
            entry_bias_grad,
            exit_bias_grad,
            second_gain_grad,
            hidden_bias_grad,
            return_bias_grad,
        ),
        ("shard", "ctx"),
    )
    return (
        result,
        tokens_grad,
        small_grads[0],
        weight_grads[0],
        small_grads[1],
        weight_grads[1],
        small_grads[2],
        small_grads[3],
        weight_grads[2],
        small_grads[4],
        weight_grads[3],
        small_grads[5],
    )


def solution(mesh):
    return jax.shard_map(
        shards,
        mesh=mesh,
        in_specs=(
            P("shard", "ctx", None),
            P("shard"),
            P(),
            P(None, ("shard", "ctx"), "tp"),
            P(None, "tp"),
            P("tp", ("shard", "ctx")),
            P(),
            P(),
            P(("shard", "ctx"), "tp"),
            P("tp"),
            P("tp", ("shard", "ctx")),
            P(),
            P("shard", "ctx", None),
        ),
        out_specs=(
            P("shard", "ctx", None),
            P("shard", "ctx", None),
            P(),
            P(None, ("shard", "ctx"), "tp"),
            P(None, "tp"),
            P("tp", ("shard", "ctx")),
            P(),
            P(),
            P(("shard", "ctx"), "tp"),
            P("tp"),
            P("tp", ("shard", "ctx")),
            P(),
        ),
        check_vma=False,
    )
```

profile of v0, /device:TPU:0, one launch (start us, length us, event | category | flops | bytes accessed | tf_op | source)
XLA Modules:
  0.0 1059.9 jit_solution(7665863335763462059)
XLA Ops:
  14.5 13.1 %all_gather.24 = bf16[3,768,192]{2,1,0:T(8,128)(2,1)S(1)} all-gather(bf16[3,96,192]{2,1,0:T(8,128)(2,1)S(1)} %copy-done.38), channel_id=1, replica_groups=mesh['shard'=2,'ctx'=4,'tp'=4] {'shard','ctx'}, dimensions={1}, use_global_device_ids=true | all-gather | bytes 995328 | tf_op jit(solution)/shard_map/all_gather | solution.py:39
  42.1 12.4 %all_gather.27 = bf16[192,768]{0,1:T(8,128)(2,1)} all-gather(bf16[192,96]{0,1:T(8,128)(2,1)} %copy.58), channel_id=1, replica_groups=mesh['shard'=2,'ctx'=4,'tp'=4] {'shard','ctx'}, dimensions={1}, use_global_device_ids=true | all-gather | bytes 331776 | tf_op jit(solution)/shard_map/all_gather | solution.py:40
  61.6 4.6 copy-done
  69.6 6.6 all-gather.5.cloned.1.call-done
  78.1 6.6 fusion.24
  89.6 4.3 copy.59
  99.9 109.4 %all-reduce.7.cloned.1.call-done = f32[1024,768]{1,0:T(8,128)} async-done(((f32[1024,768]{1,0:T(8,128)}), f32[1024,768]{1,0:T(8,128)}) %all-reduce.7.cloned.1.call-update) | async-done | bytes 3145744 | tf_op jit(solution)/shard_map/psum | solution.py:90
  211.6 4.3 multiply_reduce_fusion.4
  215.9 5.5 fusion.33
  221.4 5.6 convert_reduce_fusion.1
  232.5 119.0 %all-reduce.11.cloned.1.call-done = f32[1024,768]{1,0:T(8,128)} async-done(((f32[1024,768]{1,0:T(8,128)}), f32[1024,768]{1,0:T(8,128)}) %all-reduce.11.cloned.1.call-update) | async-done | bytes 3145744 | tf_op jit(solution)/shard_map/psum | solution.py:128
  363.4 7.6 fusion
  376.7 48.2 %copy.69 = f32[4,1024,192]{0,2,1:T(8,128)} copy(f32[4,1024,192]{1,2,0:T(8,128)S(1)} %bitcast.133) | data formatting | bytes 6291456
  424.9 84.3 %reshape.241 = f32[1024,768]{1,0:T(8,128)} reshape(f32[1024,192,4]{2,1,0:T(8,128)} %bitcast.22) | data formatting | bytes 6291456
  509.8 6.3 fusion.5
  516.1 48.3 %copy.71 = f32[4,1024,192]{0,2,1:T(8,128)} copy(f32[4,1024,192]{1,2,0:T(8,128)S(1)} %bitcast.127) | data formatting | bytes 6291456
  564.3 84.3 %reshape.243 = f32[1024,768]{1,0:T(8,128)} reshape(f32[1024,192,4]{2,1,0:T(8,128)} %bitcast.25) | data formatting | bytes 6291456
  649.9 5.1 convolution_convert_fusion.1
  657.0 5.1 convert_reduce_fusion.4
  663.8 29.2 %reshape.242 = bf16[256,192,4]{2,1,0:T(8,128)(2,1)} reshape(f32[256,768]{1,0:T(8,128)} %reduce-scatter.19.cloned.1.call-done) | data formatting | bytes 1179648
  693.0 12.2 %copy.70 = bf16[4,256,192]{1,0,2:T(4,128)(2,1)S(1)} copy(bf16[4,256,192]{0,2,1:T(8,128)(2,1)} %bitcast.123) | data formatting | bytes 786432
  705.3 29.3 %reshape.244 = bf16[256,192,4]{2,1,0:T(8,128)(2,1)} reshape(f32[256,768]{1,0:T(8,128)} %reduce-scatter.21.cloned.1.call-done) | data formatting | bytes 1179648
  734.6 12.2 %copy.72 = bf16[4,256,192]{1,0,2:T(4,128)(2,1)S(1)} copy(bf16[4,256,192]{0,2,1:T(8,128)(2,1)} %bitcast.124) | data formatting | bytes 786432
  760.4 5.8 fusion.34
  766.3 4.4 fusion.32
  774.1 3.9 copy.66
  778.1 15.8 %reduce-scatter.25.cloned.1.call-done = f32[96,192]{1,0:T(8,128)} async-done(((f32[768,192]{1,0:T(8,128)}), f32[96,192]{1,0:T(8,128)}) %reduce-scatter.25.cloned.1.call-update) | async-done | bytes 73744
  796.5 40.9 %reduce-scatter.23.cloned.1.call-done = f32[96,576]{1,0:T(8,128)} async-done(((f32[768,576]{1,0:T(8,128)}), f32[96,576]{1,0:T(8,128)}) %reduce-scatter.23.cloned.1.call-update) | async-done | bytes 221200
  839.3 121.4 %all-reduce.13.cloned.1.call-done = f32[1024,768]{1,0:T(8,128)} async-done(((f32[1024,768]{1,0:T(8,128)}), f32[1024,768]{1,0:T(8,128)}) %all-reduce.13.cloned.1.call-update) | async-done | bytes 3145744 | tf_op jit(solution)/shard_map/psum | solution.py:197
  969.2 25.0 %all-reduce.1 = (f32[768]{0:T(1024)}, f32[2,192]{1,0:T(2,128)}, f32[768]{0:T(1024)}, f32[768]{0:T(1024)}, f32[768]{0:T(1024)}, /*index=5*/f32[768]{0:T(1024)}) all-reduce(f32[768]{0:T(1024)S(1)} %get-tuple-element.48, f32[2,192]{1,0:T(2,128)S(1)} %pad_maximum_fusion.2, ...), channel_id=1, replica_groups=mesh['shard'=2,'ctx'=4,'tp'=4] {'shard','ctx'}, use_global_device_ids=true, to_apply=%region_19.20 | all-reduce | flops 4224 | bytes 33792 | tf_op jit(solution)/shard_map/psum | solution.py:211
  994.2 11.9 %reduce-scatter.17.cloned.1.call-done = f32[768,96]{0,1:T(8,128)} async-done(((f32[768,768]{0,1:T(8,128)}), f32[768,96]{0,1:T(8,128)}) %reduce-scatter.17.cloned.1.call-update) | async-done | bytes 294928 | tf_op jit(solution)/shard_map/reduce_scatter | solution.py:209
  1006.1 46.2 %reduce-scatter.15.cloned.1.call-done = f32[96,768]{1,0:T(8,128)} async-done(((f32[768,768]{1,0:T(8,128)}), f32[96,768]{1,0:T(8,128)}) %reduce-scatter.15.cloned.1.call-update) | async-done | bytes 294928 | tf_op jit(solution)/shard_map/reduce_scatter | solution.py:208
  (249 shorter events, 104.1 us)
Async XLA Ops:
  8.0 48.6 %all-gather.7.cloned.1.call-start = ((), (), s32[]{:S(2)}) async-start(), calls=%async_computation.7 | async-start | bytes 1966080 | tf_op jit(solution)/shard_map/all_gather | solution.py:58
  13.3 198.3 %copy-start.1 = (f32[4,256,767]{2,1,0:T(8,128)}, f32[4,256,767]{2,1,0:T(8,128)S(1)}, u32[]{:S(2)}) copy-start(f32[4,256,767]{2,1,0:T(8,128)S(1)} %copy.52) | copy-start | bytes 9424900
  13.3 16.2 %copy-start.45 = (f32[768]{0:T(1024)S(1)}, f32[768]{0:T(1024)}, u32[]{:S(2)}) copy-start(f32[768]{0:T(1024)} %param.15) | copy-start | bytes 9220
  14.5 15.0 %copy-start.14 = (f32[1,1024]{0,1:T(8,128)S(1)}, f32[1,1024]{0,1:T(8,128)}, u32[]{:S(2)}) copy-start(f32[1,1024]{0,1:T(8,128)} %copy.81) | copy-start | bytes 12292
  33.0 43.2 %all-gather.5.cloned.1.call-start = ((), (), s32[]{:S(2)}) async-start(), calls=%async_computation.6 | async-start | bytes 1966080 | tf_op jit(solution)/shard_map/all_gather | solution.py:59
  33.1 21.4 %copy-start.59 = (s32[4]{0:T(128)S(1)}, s32[4]{0:T(128)}, u32[]{:S(2)}) copy-start(s32[4]{0:T(128)} %param.14) | copy-start | bytes 52
  36.3 173.0 %all-reduce.7.cloned.1.call-start = ((), (), s32[]{:S(2)}) async-start(), calls=%async_computation.8 | async-start | bytes 6291456 | tf_op jit(solution)/shard_map/psum | solution.py:90
  42.0 19.5 %copy-start.26 = (bf16[4,256,3,64]{1,0,3,2:T(4,128)(2,1)}, bf16[4,256,3,64]{1,0,3,2:T(4,128)(2,1)S(1)}, u32[]{:S(2)}) copy-start(bf16[4,256,3,64]{1,0,3,2:T(4,128)(2,1)S(1)} %reshape.226) | copy-start | bytes 1179652
  61.5 16.6 %copy-start.37 = (f32[4,3,256]{2,1,0:T(4,128)}, f32[4,3,256]{2,1,0:T(4,128)S(1)}, u32[]{:S(2)}) copy-start(f32[4,3,256]{2,1,0:T(4,128)S(1)} %get-tuple-element.72) | copy-start | bytes 36868
  78.1 7.7 copy-start.30
  88.1 127.8 %all-gather.9.cloned.1.call-start = ((), (), s32[]{:S(2)}) async-start(), calls=%async_computation.9 | async-start | bytes 1327104 | tf_op jit(solution)/shard_map/all_gather | solution.py:41
  88.7 132.7 %all-gather.11.cloned.1.call-start = ((), (), s32[]{:S(2)}) async-start(), calls=%async_computation.10 | async-start | bytes 1327104 | tf_op jit(solution)/shard_map/all_gather | solution.py:42
  89.3 262.2 %all-reduce.11.cloned.1.call-start = ((), (), s32[]{:S(2)}) async-start(), calls=%async_computation.12 | async-start | bytes 6291456 | tf_op jit(solution)/shard_map/psum | solution.py:128
  96.4 112.9 %copy-start.47 = (f32[768]{0:T(1024)S(1)}, f32[768]{0:T(1024)}, u32[]{:S(2)}) copy-start(f32[768]{0:T(1024)} %param.19) | copy-start | bytes 9220
  221.4 6.8 copy-start.62
  231.2 120.2 %copy-start.6 = (f32[1024,768]{1,0:T(8,128)S(1)}, f32[1024,768]{1,0:T(8,128)}, u32[]{:S(2)}) copy-start(f32[1024,768]{1,0:T(8,128)} %get-tuple-element.67) | copy-start | bytes 9437188
  231.3 432.5 %reduce-scatter.19.cloned.1.call-start = ((), (), s32[]{:S(2)}) async-start(), calls=%async_computation.16 | async-start | bytes 3932160
  361.6 9.5 slice-start
  361.6 9.5 slice-start.1
  363.4 7.6 slice-start.2
  509.3 196.1 %reduce-scatter.21.cloned.1.call-start = ((), (), s32[]{:S(2)}) async-start(), calls=%async_computation.17 | async-start | bytes 3932160
  648.7 122.0 %all-reduce.9.cloned.1.call-start = ((), (), s32[]{:S(2)}) async-start(), calls=%async_computation.11 | async-start | bytes 3145728 | tf_op jit(solution)/shard_map/psum | solution.py:101
  655.1 138.8 %reduce-scatter.25.cloned.1.call-start = ((), (), s32[]{:S(2)}) async-start(), calls=%async_computation.19 | async-start | bytes 884736
  656.8 180.6 %reduce-scatter.23.cloned.1.call-start = ((), (), s32[]{:S(2)}) async-start(), calls=%async_computation.18 | async-start | bytes 2211840
  705.3 41.6 %copy-start.32 = (bf16[24,8,4,256]{3,1,2,0:T(8,128)(2,1)}, bf16[24,8,4,256]{3,1,2,0:T(8,128)(2,1)S(1)}, u32[]{:S(2)}) copy-start(bf16[24,8,4,256]{3,1,2,0:T(8,128)(2,1)S(1)} %copy.85) | copy-start | bytes 1179652
  755.1 205.6 %all-reduce.13.cloned.1.call-start = ((), (), s32[]{:S(2)}) async-start(), calls=%async_computation.13 | async-start | bytes 6291456 | tf_op jit(solution)/shard_map/psum | solution.py:197
  760.3 245.8 %reduce-scatter.17.cloned.1.call-start = ((), (), s32[]{:S(2)}) async-start(), calls=%async_computation.15 | async-start | bytes 2654208 | tf_op jit(solution)/shard_map/reduce_scatter | solution.py:209
  766.2 286.1 %reduce-scatter.15.cloned.1.call-start = ((), (), s32[]{:S(2)}) async-start(), calls=%async_computation.14 | async-start | bytes 2654208 | tf_op jit(solution)/shard_map/reduce_scatter | solution.py:208
  772.6 22.9 %copy-start.29 = (bf16[4,256,192]{1,0,2:T(4,128)(2,1)S(1)}, bf16[4,256,192]{1,0,2:T(4,128)(2,1)}, u32[]{:S(2)}) copy-start(bf16[4,256,192]{1,0,2:T(4,128)(2,1)} %copy-done.28) | copy-start | bytes 1179652
  774.1 186.7 %copy-start.2 = (f32[4,256,767]{2,1,0:T(8,128)S(1)}, f32[4,256,767]{2,1,0:T(8,128)}, u32[]{:S(2)}) copy-start(f32[4,256,767]{2,1,0:T(8,128)} %copy-done.1) | copy-start | bytes 9424900
  774.1 186.7 %copy-start.41 = (f32[1024]{0:T(1024)S(1)}, f32[1024]{0:T(1024)}, u32[]{:S(2)}) copy-start(f32[1024]{0:T(1024)} %copy-done.40) | copy-start | bytes 12292
  774.1 186.7 %copy-start.46 = (f32[768]{0:T(1024)S(1)}, f32[768]{0:T(1024)}, u32[]{:S(2)}) copy-start(f32[768]{0:T(1024)} %param.15) | copy-start | bytes 9220
  (51 other events, 166.1 us)
Sparse Core Ops, SparseCore 0:
  33.1 21.6 all-gather.6
  56.4 19.7 all-gather.4
  88.2 121.0 all-reduce.6
  231.4 120.0 all-reduce.10
  509.4 36.8 reduce-scatter.18
  648.8 36.3 reduce-scatter.20
  687.6 68.9 all-reduce.8
  759.7 34.0 reduce-scatter.24
  797.3 40.1 reduce-scatter.22
  839.7 121.0 all-reduce.12
  964.7 41.4 reduce-scatter.16
  1009.9 42.3 reduce-scatter.14
Sparse Core Ops, SparseCore 1:
  90.5 23.8 all-gather.8
  116.1 23.8 all-gather.10
where the time goes:
time: 1070 us; the launch traced here: 1060 us
  waiting for transfers between devices  472 us (44%)
  local copies, waits for them, and re-layouts  400 us (37%)
  matrix products  69.9 us (7%)
  blocking collectives  50.5 us (5%)
  other arithmetic  48.4 us (5%)
  between operations  16.9 us (2%)
    unnamed x161, local copies, waits for them, and re-layouts  384 us
    psum x1, waiting for transfers between devices, shards(): first_grad = lax.psum(first_part, 'tp')  121 us
    psum x1, waiting for transfers between devices, shards(): second_grad = lax.psum(second_term, 'tp')  119 us
    psum x1, waiting for transfers between devices, shards(): branch = lax.psum(exit_term, 'tp') + exit_bias  109 us
    unnamed x18, waiting for transfers between devices  58 us
    reduce_scatter x1, waiting for transfers between devices, shards(): lax.psum_scatter(hidden_weight_grad, ('shard', 'ctx'), scatter_dimension=...  46.2 us
    psum x1, blocking collectives, shards(): lax.psum((first_gain_grad, entry_bias_grad, exit_bias_grad, second_gain_g...  25 us
  transfers between devices with their start and end apart: 14, of which 8 were waited for; matrix products, arithmetic and copies ran while one was open for 30% of the time, Pallas kernels for 0%

commit v1 on v0

--- a/solution.py
+++ b/solution.py
@@ -3,6 +3,7 @@
 import jax.numpy as jnp
 from jax import lax
 from jax.sharding import PartitionSpec as P
+from jax.lax import all_gather
 
 HDIM = 64
 EPSILON = 1e-05
@@ -194,7 +195,7 @@
         + jnp.einsum("re,de->rd", key_low, full_entry[1], preferred_element_type=single)
         + jnp.einsum("re,de->rd", value_low, full_entry[2], preferred_element_type=single)
     )
-    first_grad = lax.psum(first_part, "tp")
+    first_grad = jnp.sum(all_gather(first_part, "tp"), axis=0)
     first_gain_grad = jnp.sum(first_grad * first_unit, 0)
     first_scaled = first_grad * first_gain
     stream_grad = middle_grad + first_inverse * (

time: 1070 us -> 1160 us (1.084)
  waiting for transfers between devices: 472 us -> 560 us
    all_gather x0 -> x1, waiting for transfers between devices: none -> 218 us  [shards(): first_grad = jnp.sum(all_gather(first_part, 'tp'), axis=0)]
    psum x1 -> x0, waiting for transfers between devices: 121 us -> none  [shards(): first_grad = lax.psum(first_part, 'tp')]
  transfers between devices with their start and end apart: 14 -> 14, of which waited for: 8 -> 8; matrix products, arithmetic and copies ran while one was open for 30% -> 28% of each run, Pallas kernels for 0% -> 0%
where the time goes in v1:
time: 1160 us
  waiting for transfers between devices  560 us (48%)
  local copies, waits for them, and re-layouts  400 us (34%)
  matrix products  69.8 us (6%)
  other arithmetic  56.2 us (5%)
  blocking collectives  50.8 us (4%)
  between operations  16.9 us (1%)
    unnamed x161, local copies, waits for them, and re-layouts  384 us
    all_gather x1, waiting for transfers between devices, shards(): first_grad = jnp.sum(all_gather(first_part, 'tp'), axis=0)  218 us
    psum x1, waiting for transfers between devices, shards(): second_grad = lax.psum(second_term, 'tp')  119 us
    psum x1, waiting for transfers between devices, shards(): branch = lax.psum(exit_term, 'tp') + exit_bias  109 us
    unnamed x18, waiting for transfers between devices  58.3 us
    reduce_scatter x1, waiting for transfers between devices, shards(): lax.psum_scatter(hidden_weight_grad, ('shard', 'ctx'), scatter_dimension=...  46.1 us
    psum x1, blocking collectives, shards(): lax.psum((first_gain_grad, entry_bias_grad, exit_bias_grad, second_gain_g...  25.3 us
  transfers between devices with their start and end apart: 14, of which 8 were waited for; matrix products, arithmetic and copies ran while one was open for 28% of the time, Pallas kernels for 0%

profile of v1, /device:TPU:0, one launch (start us, length us, event | category | flops | bytes accessed | tf_op | source)
XLA Modules:
  0.0 1155.6 jit_solution(5058209637562011660)
XLA Ops:
  14.5 13.1 %all_gather.30 = bf16[3,768,192]{2,1,0:T(8,128)(2,1)S(1)} all-gather(bf16[3,96,192]{2,1,0:T(8,128)(2,1)S(1)} %copy-done.38), channel_id=1, replica_groups=mesh['shard'=2,'ctx'=4,'tp'=4] {'shard','ctx'}, dimensions={1}, use_global_device_ids=true | all-gather | bytes 995328 | tf_op jit(solution)/shard_map/all_gather | solution.py:40
  42.1 12.4 %all_gather.33 = bf16[192,768]{0,1:T(8,128)(2,1)} all-gather(bf16[192,96]{0,1:T(8,128)(2,1)} %copy.58), channel_id=1, replica_groups=mesh['shard'=2,'ctx'=4,'tp'=4] {'shard','ctx'}, dimensions={1}, use_global_device_ids=true | all-gather | bytes 331776 | tf_op jit(solution)/shard_map/all_gather | solution.py:41
  61.6 4.6 copy-done
  69.6 6.6 all-gather.7.cloned.1.call-done
  78.1 6.6 fusion.24
  89.6 4.3 copy.59
  99.9 109.4 %all-reduce.6.cloned.1.call-done = f32[1024,768]{1,0:T(8,128)} async-done(((f32[1024,768]{1,0:T(8,128)}), f32[1024,768]{1,0:T(8,128)}) %all-reduce.6.cloned.1.call-update) | async-done | bytes 3145744 | tf_op jit(solution)/shard_map/psum | solution.py:91
  211.6 4.3 multiply_reduce_fusion.4
  215.9 5.5 fusion.33
  221.4 5.6 convert_reduce_fusion.1
  232.5 119.0 %all-reduce.10.cloned.1.call-done = f32[1024,768]{1,0:T(8,128)} async-done(((f32[1024,768]{1,0:T(8,128)}), f32[1024,768]{1,0:T(8,128)}) %all-reduce.10.cloned.1.call-update) | async-done | bytes 3145744 | tf_op jit(solution)/shard_map/psum | solution.py:129
  363.4 7.6 fusion
  376.7 48.2 %copy.69 = f32[4,1024,192]{0,2,1:T(8,128)} copy(f32[4,1024,192]{1,2,0:T(8,128)S(1)} %bitcast.134) | data formatting | bytes 6291456
  424.9 84.3 %reshape.242 = f32[1024,768]{1,0:T(8,128)} reshape(f32[1024,192,4]{2,1,0:T(8,128)} %bitcast.23) | data formatting | bytes 6291456
  509.8 6.3 fusion.5
  516.1 48.3 %copy.71 = f32[4,1024,192]{0,2,1:T(8,128)} copy(f32[4,1024,192]{1,2,0:T(8,128)S(1)} %bitcast.128) | data formatting | bytes 6291456
  564.3 84.3 %reshape.244 = f32[1024,768]{1,0:T(8,128)} reshape(f32[1024,192,4]{2,1,0:T(8,128)} %bitcast.26) | data formatting | bytes 6291456
  649.9 5.1 convolution_convert_fusion.1
  657.0 5.1 convert_reduce_fusion.4
  663.8 29.2 %reshape.243 = bf16[256,192,4]{2,1,0:T(8,128)(2,1)} reshape(f32[256,768]{1,0:T(8,128)} %reduce-scatter.19.cloned.1.call-done) | data formatting | bytes 1179648
  693.0 12.2 %copy.70 = bf16[4,256,192]{1,0,2:T(4,128)(2,1)S(1)} copy(bf16[4,256,192]{0,2,1:T(8,128)(2,1)} %bitcast.124) | data formatting | bytes 786432
  705.3 29.3 %reshape.245 = bf16[256,192,4]{2,1,0:T(8,128)(2,1)} reshape(f32[256,768]{1,0:T(8,128)} %reduce-scatter.21.cloned.1.call-done) | data formatting | bytes 1179648
  734.6 12.2 %copy.72 = bf16[4,256,192]{1,0,2:T(4,128)(2,1)S(1)} copy(bf16[4,256,192]{0,2,1:T(8,128)(2,1)} %bitcast.125) | data formatting | bytes 786432
  760.3 5.8 fusion.34
  766.2 4.4 fusion.32
  773.9 3.8 copy.66
  777.8 16.0 %reduce-scatter.25.cloned.1.call-done = f32[96,192]{1,0:T(8,128)} async-done(((f32[768,192]{1,0:T(8,128)}), f32[96,192]{1,0:T(8,128)}) %reduce-scatter.25.cloned.1.call-update) | async-done | bytes 73744
  796.5 40.9 %reduce-scatter.23.cloned.1.call-done = f32[96,576]{1,0:T(8,128)} async-done(((f32[768,576]{1,0:T(8,128)}), f32[96,576]{1,0:T(8,128)}) %reduce-scatter.23.cloned.1.call-update) | async-done | bytes 221200
  839.4 217.7 %all-gather.15.cloned.1.call-done = f32[4096,768]{1,0:T(8,128)} async-done(((f32[1024,768]{1,0:T(8,128)}), f32[4096,768]{1,0:T(8,128)}) %all-gather.15.cloned.1.call-update) | async-done | bytes 12582928 | tf_op jit(solution)/shard_map/all_gather | solution.py:198
  1057.1 7.6 reduce_sum.181
  1073.6 25.3 %all-reduce.1 = (f32[768]{0:T(1024)}, f32[2,192]{1,0:T(2,128)}, f32[768]{0:T(1024)}, f32[768]{0:T(1024)}, f32[768]{0:T(1024)}, /*index=5*/f32[768]{0:T(1024)}) all-reduce(f32[768]{0:T(1024)S(1)} %get-tuple-element.48, f32[2,192]{1,0:T(2,128)S(1)} %pad_maximum_fusion.2, ...), channel_id=1, replica_groups=mesh['shard'=2,'ctx'=4,'tp'=4] {'shard','ctx'}, use_global_device_ids=true, to_apply=%region_19.20 | all-reduce | flops 4224 | bytes 33792 | tf_op jit(solution)/shard_map/psum | solution.py:212
  1101.8 46.1 %reduce-scatter.15.cloned.1.call-done = f32[96,768]{1,0:T(8,128)} async-done(((f32[768,768]{1,0:T(8,128)}), f32[96,768]{1,0:T(8,128)}) %reduce-scatter.15.cloned.1.call-update) | async-done | bytes 294928 | tf_op jit(solution)/shard_map/reduce_scatter | solution.py:209
  (250 shorter events, 107.4 us)
Async XLA Ops:
  8.0 48.6 %all-gather.9.cloned.1.call-start = ((), (), s32[]{:S(2)}) async-start(), calls=%async_computation.7 | async-start | bytes 1966080 | tf_op jit(solution)/shard_map/all_gather | solution.py:59
  13.3 198.3 %copy-start.1 = (f32[4,256,767]{2,1,0:T(8,128)}, f32[4,256,767]{2,1,0:T(8,128)S(1)}, u32[]{:S(2)}) copy-start(f32[4,256,767]{2,1,0:T(8,128)S(1)} %copy.52) | copy-start | bytes 9424900
  13.3 16.2 %copy-start.45 = (f32[768]{0:T(1024)S(1)}, f32[768]{0:T(1024)}, u32[]{:S(2)}) copy-start(f32[768]{0:T(1024)} %param.15) | copy-start | bytes 9220
  14.5 15.0 %copy-start.15 = (f32[1,1024]{0,1:T(8,128)S(1)}, f32[1,1024]{0,1:T(8,128)}, u32[]{:S(2)}) copy-start(f32[1,1024]{0,1:T(8,128)} %copy.81) | copy-start | bytes 12292
  33.0 43.2 %all-gather.7.cloned.1.call-start = ((), (), s32[]{:S(2)}) async-start(), calls=%async_computation.6 | async-start | bytes 1966080 | tf_op jit(solution)/shard_map/all_gather | solution.py:60
  33.1 21.4 %copy-start.59 = (s32[4]{0:T(128)S(1)}, s32[4]{0:T(128)}, u32[]{:S(2)}) copy-start(s32[4]{0:T(128)} %param.14) | copy-start | bytes 52
  36.3 173.0 %all-reduce.6.cloned.1.call-start = ((), (), s32[]{:S(2)}) async-start(), calls=%async_computation.8 | async-start | bytes 6291456 | tf_op jit(solution)/shard_map/psum | solution.py:91
  42.0 19.5 %copy-start.26 = (bf16[4,256,3,64]{1,0,3,2:T(4,128)(2,1)}, bf16[4,256,3,64]{1,0,3,2:T(4,128)(2,1)S(1)}, u32[]{:S(2)}) copy-start(bf16[4,256,3,64]{1,0,3,2:T(4,128)(2,1)S(1)} %reshape.226) | copy-start | bytes 1179652
  61.5 16.6 %copy-start.37 = (f32[4,3,256]{2,1,0:T(4,128)}, f32[4,3,256]{2,1,0:T(4,128)S(1)}, u32[]{:S(2)}) copy-start(f32[4,3,256]{2,1,0:T(4,128)S(1)} %get-tuple-element.72) | copy-start | bytes 36868
  78.1 7.7 copy-start.30
  88.1 127.8 %all-gather.11.cloned.1.call-start = ((), (), s32[]{:S(2)}) async-start(), calls=%async_computation.9 | async-start | bytes 1327104 | tf_op jit(solution)/shard_map/all_gather | solution.py:42
  88.7 132.7 %all-gather.13.cloned.1.call-start = ((), (), s32[]{:S(2)}) async-start(), calls=%async_computation.10 | async-start | bytes 1327104 | tf_op jit(solution)/shard_map/all_gather | solution.py:43
  89.3 262.2 %all-reduce.10.cloned.1.call-start = ((), (), s32[]{:S(2)}) async-start(), calls=%async_computation.12 | async-start | bytes 6291456 | tf_op jit(solution)/shard_map/psum | solution.py:129
  96.4 112.9 %copy-start.47 = (f32[768]{0:T(1024)S(1)}, f32[768]{0:T(1024)}, u32[]{:S(2)}) copy-start(f32[768]{0:T(1024)} %param.19) | copy-start | bytes 9220
  221.4 6.8 copy-start.62
  231.2 120.2 %copy-start.6 = (f32[1024,768]{1,0:T(8,128)S(1)}, f32[1024,768]{1,0:T(8,128)}, u32[]{:S(2)}) copy-start(f32[1024,768]{1,0:T(8,128)} %get-tuple-element.67) | copy-start | bytes 9437188
  231.3 432.5 %reduce-scatter.19.cloned.1.call-start = ((), (), s32[]{:S(2)}) async-start(), calls=%async_computation.16 | async-start | bytes 3932160
  361.6 9.5 slice-start
  361.6 9.5 slice-start.1
  363.4 7.6 slice-start.2
  509.3 196.1 %reduce-scatter.21.cloned.1.call-start = ((), (), s32[]{:S(2)}) async-start(), calls=%async_computation.17 | async-start | bytes 3932160
  648.7 121.9 %all-reduce.8.cloned.1.call-start = ((), (), s32[]{:S(2)}) async-start(), calls=%async_computation.11 | async-start | bytes 3145728 | tf_op jit(solution)/shard_map/psum | solution.py:102
  655.1 138.8 %reduce-scatter.25.cloned.1.call-start = ((), (), s32[]{:S(2)}) async-start(), calls=%async_computation.19 | async-start | bytes 884736
  656.8 180.7 %reduce-scatter.23.cloned.1.call-start = ((), (), s32[]{:S(2)}) async-start(), calls=%async_computation.18 | async-start | bytes 2211840
  705.3 41.6 %copy-start.32 = (bf16[24,8,4,256]{3,1,2,0:T(8,128)(2,1)}, bf16[24,8,4,256]{3,1,2,0:T(8,128)(2,1)S(1)}, u32[]{:S(2)}) copy-start(bf16[24,8,4,256]{3,1,2,0:T(8,128)(2,1)S(1)} %copy.85) | copy-start | bytes 1179652
  755.1 302.0 %all-gather.15.cloned.1.call-start = ((), (), s32[]{:S(2)}) async-start(), calls=%async_computation.15 | async-start | bytes 15728640 | tf_op jit(solution)/shard_map/all_gather | solution.py:198
  760.3 341.5 %reduce-scatter.17.cloned.1.call-start = ((), (), s32[]{:S(2)}) async-start(), calls=%async_computation.14 | async-start | bytes 2654208 | tf_op jit(solution)/shard_map/reduce_scatter | solution.py:210
  766.1 381.8 %reduce-scatter.15.cloned.1.call-start = ((), (), s32[]{:S(2)}) async-start(), calls=%async_computation.13 | async-start | bytes 2654208 | tf_op jit(solution)/shard_map/reduce_scatter | solution.py:209
  773.9 21.6 %copy-start.29 = (bf16[4,256,192]{1,0,2:T(4,128)(2,1)S(1)}, bf16[4,256,192]{1,0,2:T(4,128)(2,1)}, u32[]{:S(2)}) copy-start(bf16[4,256,192]{1,0,2:T(4,128)(2,1)} %copy-done.28) | copy-start | bytes 1179652
  1057.1 7.6 copy-start.2
  1057.1 7.6 copy-start.41
  1057.1 7.6 copy-start.46
  (51 other events, 168.0 us)
Sparse Core Ops, SparseCore 0:
  33.1 21.6 all-gather.8
  56.4 19.7 all-gather.6
  88.2 121.0 all-reduce.5
  231.4 120.0 all-reduce.9
  509.4 36.8 reduce-scatter.18
  648.8 36.3 reduce-scatter.20
  687.6 68.9 all-reduce.7
  759.7 34.0 reduce-scatter.24
  797.3 40.1 reduce-scatter.22
  838.9 218.1 all-gather.14
  1061.0 40.7 reduce-scatter.16
  1105.6 42.3 reduce-scatter.14
Sparse Core Ops, SparseCore 1:
  90.5 23.8 all-gather.10
  116.1 23.8 all-gather.12
